TPU v7x, 128 devices: a whole 4x4x4 slice. The times are simulated.
128 devices in a mesh: fsdp: 4 (over x_hi, core), ctx: 32 (over y, z, x_lo).
Axes of the slice: x: 4 (x_hi: 2, x_lo: 2; x = x_hi * 2 + x_lo), y: 4, z: 4, core: 2. Of those that a mesh axis runs over, the one named last changes fastest.
Arguments:
- query_branch: bfloat16 [4, 8192, 4096], P('fsdp', 'ctx'), may hold values from -6 to 6
- key_branch: bfloat16 [4, 8192, 4096], P('fsdp', 'ctx'), may hold values from -6 to 6
- value_branch: bfloat16 [4, 8192, 4096], P('fsdp', 'ctx'), may hold values from -6 to 6
- cotangent: bfloat16 [4, 8192, 4096], P('fsdp', 'ctx'), may hold values from -6 to 6
- quantized_weight_codes: int32 [4096, 4096], P('ctx', 'fsdp'), may hold values from 0 to 15
- scale_code_bytes: int32 [4096, 64], P('ctx', 'fsdp'), may hold values from 0 to 255
- row_scale_second: float32 [4096], P('ctx'), may hold values from 0.01 to 0.1
- filters: bfloat16 [256, 128], replicated, may hold values from -0.5 to 0.5
- channel_skip_weight: float32 [4096], replicated, may hold values from -6 to 6
- adapter_down_weight: bfloat16 [4096, 64], P('ctx'), may hold values from -0.09375 to 0.09375
- adapter_up_weight: bfloat16 [64, 4096], P(None, 'fsdp'), may hold values from -0.75 to 0.75
Outputs:
- output: bfloat16 [4, 8192, 4096], P('fsdp', 'ctx')
- grad_query: bfloat16 [4, 8192, 4096], P('fsdp', 'ctx')
- grad_key: bfloat16 [4, 8192, 4096], P('fsdp', 'ctx')
- grad_value: bfloat16 [4, 8192, 4096], P('fsdp', 'ctx')
- grad_down: bfloat16 [4096, 64], P('ctx')
- grad_up: bfloat16 [64, 4096], P(None, 'fsdp')
All inputs are finite; a program needn't handle non-finite values.
Results may differ from a plain program's by a relative error of at most 0.0067.
Values may be sent and summed in bfloat16 or wider, within the bound.
No kernel may reach another device: no remote copies, remote signals or barrier semaphores. Data moves between devices by JAX's collectives and lax.ppermute only.
A program may use at most 256 MiB of HBM per device.

v0:
```python
import math
import jax
import jax.numpy as jnp
from jax import lax
from jax.sharding import PartitionSpec as P

QBLOCK = 64
normal_levels = (
    -1.0,
    -0.6961928009986877,
    -0.5250730514526367,
    -0.39491748809814453,
    -0.28444138169288635,
    -0.18477343022823334,
    -0.09105003625154495,
    0.0,
    0.07958029955625534,
    0.16093020141124725,
    0.24611230194568634,
    0.33791524171829224,
    0.44070982933044434,
    0.5626170039176941,
    0.7229568362236023,
    1.0,
)
adapter_scale = 0.25


def from_behind(shard, axis, by):
    count = lax.axis_size(axis)
    pairs = [(i, i + by) for i in range(count) if 0 <= i + by < count]
    return lax.ppermute(shard, axis, pairs)


def dequantize(quantized_weight_codes, scale_code_bytes, row_scale_second):
    levels = jnp.zeros(quantized_weight_codes.shape, jnp.float32)
    for number in range(16):
        levels = jnp.where(quantized_weight_codes == number, normal_levels[number], levels)
    absmax = row_scale_second[:, None] * (scale_code_bytes.astype(jnp.float32) + 1.0) / 256.0
    absmax = jnp.repeat(absmax, QBLOCK, axis=1)
    return (levels * absmax).astype(jnp.bfloat16)


def toeplitz(filter_taps, filter_len):
    groups = filter_taps.shape[0]
    padded = jnp.concatenate([filter_taps, jnp.zeros((groups, filter_len), filter_taps.dtype)], 1)
    repeated = jnp.tile(padded, (1, filter_len))[:, : filter_len * (2 * filter_len - 1)]
    return repeated.reshape(groups, filter_len, 2 * filter_len - 1)


def block_conv(extended, toep, filter_len):
    row_count = extended.shape[0] - (filter_len - 1)
    blocks = row_count // filter_len
    current = extended[:row_count].reshape(blocks, filter_len, -1)
    following = jnp.concatenate(
        [extended[filter_len:], jnp.zeros((1, extended.shape[1]), extended.dtype)], 0
    )
    following = following.reshape(blocks, filter_len, -1)[:, : filter_len - 1]
    windows = jnp.concatenate([current, following], 1)
    windows = windows.reshape(blocks, 2 * filter_len - 1, toep.shape[0], -1)
    result = jnp.einsum("gts,bsgk->btgk", toep, windows, preferred_element_type=jnp.float32)
    return result.reshape(row_count, -1)


def local(
    query_branch,
    key_branch,
    value_branch,
    cotangent,
    quantized_weight_codes,
    scale_code_bytes,
    row_scale_second,
    filters,
    channel_skip_weight,
    adapter_down_weight,
    adapter_up_weight,
):
    filter_len = filters.shape[1]
    queries = query_branch[0]
    output_gradient = cotangent[0]
    row_count, channels = queries.shape
    token_count = query_branch.shape[0] * row_count * lax.axis_size("ctx") * lax.axis_size("fsdp")
    multiplier = adapter_scale / math.sqrt(token_count)
    query_float = queries.astype(jnp.float32)
    key_float = key_branch[0].astype(jnp.float32)
    value_float = value_branch[0].astype(jnp.float32)
    mixed = (key_float * value_float).astype(jnp.bfloat16)
    before = from_behind(mixed[row_count - (filter_len - 1) :], "ctx", 1)
    ahead_toep = toeplitz(jnp.flip(filters, 1), filter_len)
    back_toep = toeplitz(filters, filter_len)
    gated = block_conv(
        jnp.concatenate([before, mixed], 0), ahead_toep, filter_len
    ) + channel_skip_weight * mixed.astype(jnp.float32)
    gated_signal = (query_float * gated).astype(jnp.bfloat16)
    local_piece = dequantize(quantized_weight_codes, scale_code_bytes, row_scale_second)
    local_rows, up_complete = (
        lax.all_gather(local_piece, "fsdp", axis=1, tiled=True),
        lax.all_gather(adapter_up_weight, "fsdp", axis=1, tiled=True),
    )
    backward_up_term = jnp.einsum(
        "td,rd->tr", output_gradient, up_complete, preferred_element_type=jnp.float32
    ).astype(jnp.bfloat16)
    weight_rows = lax.all_gather(local_rows, "ctx", axis=0, tiled=True)
    rank_rows = lax.all_gather(adapter_down_weight, "ctx", axis=0, tiled=True)
    output_total = jnp.dot(gated_signal, weight_rows, preferred_element_type=jnp.float32)
    down_sum = jnp.dot(gated_signal, rank_rows, preferred_element_type=jnp.float32)
    elementwise_product = jnp.einsum(
        "td,cd->tc", output_gradient, weight_rows, preferred_element_type=jnp.float32
    )
    elementwise_product = elementwise_product + adapter_scale * jnp.einsum(
        "tr,cr->tc", backward_up_term, rank_rows, preferred_element_type=jnp.float32
    )
    down_projection = down_sum.astype(jnp.bfloat16)
    output = (
        output_total
        + adapter_scale * jnp.dot(down_projection, up_complete, preferred_element_type=jnp.float32)
    ).astype(jnp.bfloat16)
    grad_query = (elementwise_product * gated).astype(jnp.bfloat16)
    grad_gated = (elementwise_product * query_float).astype(jnp.bfloat16)
    leading = jnp.concatenate(
        [jnp.zeros((filter_len, channels), jnp.bfloat16), grad_gated[: filter_len - 1]], 0
    )
    spill = block_conv(leading, back_toep, filter_len)
    arrived = from_behind(spill[1:], "ctx", -1)
    tail_rows = jnp.concatenate(
        [grad_gated, jnp.zeros((filter_len - 1, channels), jnp.bfloat16)], 0
    )
    local_grad = block_conv(tail_rows, back_toep, filter_len)
    local_grad = local_grad + jnp.concatenate(
        [jnp.zeros((row_count - filter_len + 1, channels), jnp.float32), arrived], 0
    )
    grad_mixed = local_grad + channel_skip_weight * grad_gated.astype(jnp.float32)
    grad_key = (grad_mixed * value_float).astype(jnp.bfloat16)
    grad_value = (grad_mixed * key_float).astype(jnp.bfloat16)
    term_down = multiplier * jnp.einsum(
        "tc,tr->cr", gated_signal, backward_up_term, preferred_element_type=jnp.float32
    )
    term_up = multiplier * jnp.einsum(
        "tr,td->rd", down_projection, output_gradient, preferred_element_type=jnp.float32
    )
    total_down = lax.psum(term_down, "fsdp")
    grad_down = lax.psum_scatter(total_down, "ctx", scatter_dimension=0, tiled=True)
    total_up = lax.psum(term_up, "ctx")
    grad_up = lax.psum_scatter(total_up, "fsdp", scatter_dimension=1, tiled=True)
    return (
        output[None],
        grad_query[None],
        grad_key[None],
        grad_value[None],
        grad_down.astype(jnp.bfloat16),
        grad_up.astype(jnp.bfloat16),
    )


def solution(mesh):
    return jax.shard_map(
        local,
        mesh=mesh,
        in_specs=(
            P("fsdp", "ctx", None),
            P("fsdp", "ctx", None),
            P("fsdp", "ctx", None),
            P("fsdp", "ctx", None),
            P("ctx", "fsdp"),
            P("ctx", "fsdp"),
            P("ctx"),
            P(),
            P(),
            P("ctx", None),
            P(None, "fsdp"),
        ),
        out_specs=(
            P("fsdp", "ctx", None),
            P("fsdp", "ctx", None),
            P("fsdp", "ctx", None),
            P("fsdp", "ctx", None),
            P("ctx", None),
            P(None, "fsdp"),
        ),
        check_vma=False,
    )
```

profile of v0, /device:TPU:1, one launch (start us, length us, event | category | flops | bytes accessed | tf_op | source)
XLA Modules:
  0.0 1086.2 jit_solution(9586040226539737358)
XLA Ops:
  10.7 24.5 %all-gather.3.cloned.1.call-done = bf16[128,4096]{0,1:T(8,128)(2,1)} async-done(((bf16[128,1024]{0,1:T(8,128)(2,1)}), bf16[128,4096]{0,1:T(8,128)(2,1)}) %all-gather.3.cloned.1.call-update) | async-done | bytes 1048592 | tf_op jit(solution)/shard_map/all_gather | solution.py:97
  35.2 3.0 fusion.11
  38.3 1.5 slice.49
  39.8 3.2 collective-permute-start
  42.9 1.8 slice.50
  46.3 41.7 %copy.62 = bf16[32,8,128,256]{3,1,2,0:T(8,128)(2,1)S(1)} copy(bf16[32,8,128,256]{3,2,1,0:T(8,128)(2,1)S(1)} %bitcast.101) | data formatting | bytes 33554432
  88.0 6.6 slice.54
  94.6 56.8 %reshape.84 = bf16[256,128,255,1]{2,1,0,3:T(8,128)(2,1)} reshape(bf16[256,32640]{1,0:T(8,128)(2,1)} %slice.54) | data formatting | bytes 33423360 | tf_op jit(solution)/shard_map/reshape | solution.py:48
  151.3 56.7 %reshape.76 = bf16[256,128,255]{2,1,0:T(8,128)(2,1)} reshape(bf16[256,32640]{1,0:T(8,128)(2,1)} %slice.54) | data formatting | bytes 33423360 | tf_op jit(solution)/shard_map/reshape | solution.py:48
  209.3 41.7 %copy.60 = bf16[32,8,128,256]{3,1,2,0:T(8,128)(2,1)S(1)} copy(bf16[32,8,128,256]{3,2,1,0:T(8,128)(2,1)S(1)} %bitcast.102) | data formatting | bytes 33554432
  251.0 6.6 slice.52
  257.6 56.8 %reshape.83 = bf16[256,128,255,1]{2,1,0,3:T(8,128)(2,1)} reshape(bf16[256,32640]{1,0:T(8,128)(2,1)} %slice.52) | data formatting | bytes 33423360 | tf_op jit(solution)/shard_map/reshape | solution.py:48
  314.4 3.2 concatenate.45
  317.6 4.2 copy.57
  321.8 12.4 %all_gather.15 = bf16[64,4096]{1,0:T(8,128)(2,1)S(1)} all-gather(bf16[64,1024]{1,0:T(8,128)(2,1)S(1)} %copy-done.11), channel_id=1, replica_groups=mesh['fsdp'=4,'ctx'=32] {'fsdp'}, dimensions={1}, use_global_device_ids=true | all-gather | bytes 655360 | tf_op jit(solution)/shard_map/all_gather | solution.py:98
  334.1 80.4 %all_gather.14 = bf16[4096,64]{0,1:T(8,128)(2,1)S(1)} all-gather(bf16[128,64]{0,1:T(8,128)(2,1)S(1)} %copy-done.13), channel_id=1, replica_groups=mesh['fsdp'=4,'ctx'=32] {'ctx'}, dimensions={0}, use_global_device_ids=true | all-gather | bytes 540672 | tf_op jit(solution)/shard_map/all_gather | solution.py:104
  415.3 2.9 pad_maximum_fusion
  418.2 4.1 copy.23
  422.3 4.0 concatenate.44
  426.3 3.4 copy.25
  429.7 9.5 fusion.19
  439.2 2.2 copy.27
  441.3 2.2 copy.73
  443.6 5.7 copy.28
  449.2 329.5 %all-gather.5.cloned.1.call-done = bf16[4096,4096]{0,1:T(8,128)(2,1)} async-done(((bf16[128,4096]{0,1:T(8,128)(2,1)}), bf16[4096,4096]{0,1:T(8,128)(2,1)}) %all-gather.5.cloned.1.call-update) | async-done | bytes 33554448 | tf_op jit(solution)/shard_map/all_gather | solution.py:103
  778.8 17.2 %convolution_bitcast_fusion = f32[256,4096]{1,0:T(8,128)} fusion(bf16[4096,4096]{0,1:T(8,128)(2,1)} %all-gather.5.cloned.1.call-done, bf16[1,256,4096]{2,1,0:T(8,128)(2,1)S(1)} %copy-done), kind=kOutput, calls=%fused_computation.4 | convolution fusion | flops 8589934592 | bytes 39845888 | tf_op jit(solution)/shard_map/td,cd->tc/dot_general | solution.py:107
  796.0 6.7 fusion.29
  806.5 2.3 fusion.39
  808.9 2.3 copy.59
  811.2 2.8 concatenate.56.clone
  814.0 12.6 %convolution_bitcast_fusion.1 = f32[1,128,256,16]{1,3,2,0:T(8,128)} fusion(bf16[255,256,16]{0,2,1:T(8,128)(2,1)} %bitcast.111, bf16[256,128,255]{2,1,0:T(8,128)(2,1)} %reshape.76), kind=kOutput, calls=%fused_computation.45 | convolution fusion | flops 267386880 | bytes 20897792 | tf_op jit(solution)/shard_map/gts,bsgk->btgk/dot_general | solution.py:61
  826.6 3.7 slice.57
  830.3 3.0 copy.52
  834.5 3.1 convolution_multiply_fusion.2
  837.6 17.7 %fusion.43 = f32[256,4096]{1,0:T(8,128)} fusion(bf16[256,4096]{1,0:T(8,128)(2,1)} %copy-done.6, bf16[4096,4096]{0,1:T(8,128)(2,1)} %all-gather.5.cloned.1.call-done), kind=kOutput, calls=%fused_computation.55 | convolution fusion | flops 8589934592 | bytes 39845888 | tf_op jit(solution)/shard_map/dot_general | solution.py:105
  855.3 4.1 copy.46
  859.4 4.0 concatenate.49
  863.3 3.3 copy.48
  866.9 1.5 concatenate.51
  868.3 4.2 copy.58
  872.5 9.9 fusion.24
  882.4 2.2 copy.50
  884.6 2.3 copy.72
  886.9 5.7 copy.53
  892.5 4.4 fusion.7
  896.9 6.5 fusion.30
  903.4 135.5 %all-reduce.8 = bf16[64,1024]{1,0:T(8,128)(2,1)} all-reduce(f32[64,1024]{1,0:T(8,128)} %reduce-scatter.5.cloned.1.call-done), channel_id=1, replica_groups=mesh['fsdp'=4,'ctx'=32] {'ctx'}, use_global_device_ids=true, to_apply=%region_2.3 | all-reduce | flops 65536 | bytes 393216 | tf_op jit(solution)/shard_map/psum | solution.py:143
  1038.9 40.4 %psum.16 = bf16[128,64]{0,1:T(8,128)(2,1)} all-reduce(f32[128,64]{0,1:T(8,128)} %reduce-scatter.3.cloned.1.call-done), channel_id=1, replica_groups=mesh['fsdp'=4,'ctx'=32] {'fsdp'}, use_global_device_ids=true, to_apply=%region_0.1 | all-reduce | flops 8192 | bytes 49152 | tf_op jit(solution)/shard_map/psum | solution.py:141
  (55 shorter events, 12.4 us)
Async XLA Ops:
  7.2 407.4 %copy-start = (bf16[1,256,4096]{2,1,0:T(8,128)(2,1)S(1)}, bf16[1,256,4096]{2,1,0:T(8,128)(2,1)}, u32[]{:S(2)}) copy-start(bf16[1,256,4096]{2,1,0:T(8,128)(2,1)} %param.14) | copy-start | bytes 6291460
  7.2 28.0 %all-gather.3.cloned.1.call-start = ((), (), s32[]{:S(2)}) async-start(), calls=%async_computation.2 | async-start | bytes 1310720 | tf_op jit(solution)/shard_map/all_gather | solution.py:97
  10.6 768.1 %all-gather.5.cloned.1.call-start = ((), (), s32[]{:S(2)}) async-start(), calls=%async_computation.3 | async-start | bytes 34603008 | tf_op jit(solution)/shard_map/all_gather | solution.py:103
  35.2 868.2 %reduce-scatter.5.cloned.1.call-start = ((), (), s32[]{:S(2)}) async-start(), calls=%async_computation.5 | async-start | bytes 1310720 | tf_op jit(solution)/shard_map/reduce_scatter | solution.py:144
  38.2 4.7 copy-start.3
  38.2 6.5 copy-start.10
  39.8 375.6 %collective-permute-start = (bf16[127,4096]{1,0:T(8,128)(2,1)}, bf16[127,4096]{1,0:T(8,128)(2,1)}, u32[]{:S(2)}, u32[]{:S(2)}) collective-permute-start(bf16[127,4096]{1,0:T(8,128)(2,1)} %slice.49), channel_id=1, source_target_pairs={{0,1},{1,2},{2,3},{3,4},{4,5},{5,6},{6,7},{7,8},{8,9},{9,10},{10,1... | collective-permute-start | bytes 3121160 | tf_op jit(solution)/shard_map/ppermute | solution.py:32
  314.4 7.4 copy-start.11
  314.4 19.7 %copy-start.13 = (bf16[128,64]{0,1:T(8,128)(2,1)S(1)}, bf16[128,64]{0,1:T(8,128)(2,1)}, u32[]{:S(2)}) copy-start(bf16[128,64]{0,1:T(8,128)(2,1)} %param.20) | copy-start | bytes 49156
  321.8 93.6 %copy-start.4 = (bf16[256,4096]{1,0:T(8,128)(2,1)S(1)}, bf16[256,4096]{1,0:T(8,128)(2,1)}, u32[]{:S(2)}) copy-start(bf16[256,4096]{1,0:T(8,128)(2,1)} %copy-done.3) | copy-start | bytes 6291460
  426.3 3.4 copy-start.7
  449.2 346.7 %copy-start.12 = (f32[4096]{0:T(1024)S(1)}, f32[4096]{0:T(1024)}, u32[]{:S(2)}) copy-start(f32[4096]{0:T(1024)} %param.19) | copy-start | bytes 49156
  778.8 17.2 %copy-start.5 = (bf16[256,4096]{1,0:T(8,128)(2,1)S(1)}, bf16[256,4096]{1,0:T(8,128)(2,1)}, u32[]{:S(2)}) copy-start(bf16[256,4096]{1,0:T(8,128)(2,1)} %copy-done.3) | copy-start | bytes 6291460
  778.8 17.2 %copy-start.9 = (f32[256,4096]{1,0:T(8,128)S(1)}, f32[256,4096]{1,0:T(8,128)}, u32[]{:S(2)}) copy-start(f32[256,4096]{1,0:T(8,128)} %copy.28) | copy-start | bytes 12582916
  802.7 1.3 copy-start.6
  802.7 3.8 copy-start.14
  806.2 232.7 %reduce-scatter.3.cloned.1.call-start = ((), (), s32[]{:S(2)}) async-start(), calls=%async_computation.4 | async-start | bytes 1081344 | tf_op jit(solution)/shard_map/reduce_scatter | solution.py:142
  833.2 63.7 %collective-permute-start.1 = (f32[127,4096]{1,0:T(8,128)}, f32[127,4096]{1,0:T(8,128)}, u32[]{:S(2)}, u32[]{:S(2)}) collective-permute-start(f32[127,4096]{1,0:T(8,128)} %copy.52), channel_id=1, source_target_pairs={{1,0},{2,1},{3,2},{4,3},{5,4},{6,5},{7,6},{8,7},{9,8},{10,9},{11,1... | collective-permute-start | bytes 6242312 | tf_op jit(solution)/shard_map/ppermute | solution.py:32
  863.3 3.3 copy-start.1
  892.5 4.4 copy-start.2
  892.5 4.4 copy-start.8
Sparse Core Ops, SparseCore 0:
  10.8 24.3 all-gather.2
  36.7 742.0 all-gather.4
  806.4 30.7 reduce-scatter.4
  839.4 139.4 reduce-scatter.2
where the time goes:
time: 1100 us; the launch traced here: 1090 us
  waiting for transfers between devices  354 us (32%)
  local copies, waits for them, and re-layouts  344 us (31%)
  blocking collectives  269 us (24%)
  matrix products  84 us (8%)
  other arithmetic  16.8 us (2%)
  between operations  14.3 us (1%)
    all_gather x1, waiting for transfers between devices, local(): weight_rows = lax.all_gather(local_rows, 'ctx', axis=0, tiled=True)  330 us
    reshape x3, local copies, waits for them, and re-layouts, toeplitz(): return repeated.reshape(groups, filter_len, 2 * filter_len - 1)  170 us
    psum x1, blocking collectives, local(): total_up = lax.psum(term_up, 'ctx')  135 us
    unnamed x38, local copies, waits for them, and re-layouts  101 us
    all_gather x1, blocking collectives, local(): rank_rows = lax.all_gather(adapter_down_weight, 'ctx', axis=0, tiled=True)  80.4 us
    psum x1, blocking collectives, local(): total_down = lax.psum(term_down, 'fsdp')  40.4 us
    dot_general x3, matrix products, block_conv(): jnp.einsum('gts,bsgk->btgk', toep, windows, preferred_element_type=jnp.fl...  32 us
    all_gather x1, waiting for transfers between devices, local(): lax.all_gather(local_piece, 'fsdp', axis=1, tiled=True)  24.5 us
  transfers between devices with their start and end apart: 6, of which 2 were waited for; matrix products, arithmetic and copies ran while one was open for 38% of the time, Pallas kernels for 0%

commit v1 on v0

--- a/solution.py
+++ b/solution.py
@@ -138,7 +138,8 @@
     term_up = multiplier * jnp.einsum(
         "tr,td->rd", down_projection, output_gradient, preferred_element_type=jnp.float32
     )
-    total_down = lax.psum(term_down, "fsdp")
+    parts = lax.all_gather(term_down, "fsdp")
+    total_down = jnp.sum(parts, axis=0)
     grad_down = lax.psum_scatter(total_down, "ctx", scatter_dimension=0, tiled=True)
     total_up = lax.psum(term_up, "ctx")
     grad_up = lax.psum_scatter(total_up, "fsdp", scatter_dimension=1, tiled=True)

time: 1100 us -> 1250 us (1.14)
  the two profiles are of different devices: /device:TPU:1 before, /device:TPU:0 now
where the time goes in v1:
time: 1250 us
  waiting for transfers between devices  505 us (40%)
  local copies, waits for them, and re-layouts  350 us (28%)
  blocking collectives  265 us (21%)
  matrix products  84.2 us (7%)
  other arithmetic  24 us (2%)
  between operations  14.3 us (1%)
    all_gather x1, waiting for transfers between devices, local(): weight_rows = lax.all_gather(local_rows, 'ctx', axis=0, tiled=True)  482 us
    reshape x3, local copies, waits for them, and re-layouts, toeplitz(): return repeated.reshape(groups, filter_len, 2 * filter_len - 1)  170 us
    psum x1, blocking collectives, local(): total_up = lax.psum(term_up, 'ctx')  162 us
    unnamed x42, local copies, waits for them, and re-layouts  101 us
    all_gather x1, blocking collectives, local(): rank_rows = lax.all_gather(adapter_down_weight, 'ctx', axis=0, tiled=True)  91.4 us
    dot_general x3, matrix products, block_conv(): jnp.einsum('gts,bsgk->btgk', toep, windows, preferred_element_type=jnp.fl...  31.6 us
  transfers between devices with their start and end apart: 7, of which 2 were waited for; matrix products, arithmetic and copies ran while one was open for 34% of the time, Pallas kernels for 0%

profile of v1, /device:TPU:0, one launch (start us, length us, event | category | flops | bytes accessed | tf_op | source)
XLA Modules:
  0.0 1247.9 jit_solution(10605540162486815227)
XLA Ops:
  10.7 23.3 %all-gather.5.cloned.1.call-done = bf16[128,4096]{0,1:T(8,128)(2,1)} async-done(((bf16[128,1024]{0,1:T(8,128)(2,1)}), bf16[128,4096]{0,1:T(8,128)(2,1)}) %all-gather.5.cloned.1.call-update) | async-done | bytes 1048592 | tf_op jit(solution)/shard_map/all_gather | solution.py:97
  34.1 3.0 fusion.11
  37.1 1.5 slice.49
  38.6 3.4 collective-permute-start
  42.0 1.8 slice.50
  45.4 41.7 %copy.60 = bf16[32,8,128,256]{3,1,2,0:T(8,128)(2,1)S(1)} copy(bf16[32,8,128,256]{3,2,1,0:T(8,128)(2,1)S(1)} %bitcast.103) | data formatting | bytes 33554432
  87.1 6.6 slice.52
  93.7 56.8 %reshape.84 = bf16[256,128,255,1]{2,1,0,3:T(8,128)(2,1)} reshape(bf16[256,32640]{1,0:T(8,128)(2,1)} %slice.52) | data formatting | bytes 33423360 | tf_op jit(solution)/shard_map/reshape | solution.py:48
  150.4 3.2 concatenate.45
  153.6 4.1 copy.57
  157.8 12.0 all_gather.21
  169.7 91.4 %all_gather.20 = bf16[4096,64]{0,1:T(8,128)(2,1)S(1)} all-gather(bf16[128,64]{0,1:T(8,128)(2,1)S(1)} %copy-done.15), channel_id=1, replica_groups=mesh['fsdp'=4,'ctx'=32] {'ctx'}, dimensions={0}, use_global_device_ids=true | all-gather | bytes 540672 | tf_op jit(solution)/shard_map/all_gather | solution.py:104
  261.9 2.9 pad_maximum_fusion
  264.8 4.1 copy.23
  268.9 4.0 concatenate.44
  272.9 3.3 copy.25
  276.2 9.5 fusion.19
  285.7 2.2 copy.27
  287.9 2.3 copy.73
  290.2 5.7 copy.28
  295.8 482.0 %all-gather.7.cloned.1.call-done = bf16[4096,4096]{0,1:T(8,128)(2,1)} async-done(((bf16[128,4096]{0,1:T(8,128)(2,1)}), bf16[4096,4096]{0,1:T(8,128)(2,1)}) %all-gather.7.cloned.1.call-update) | async-done | bytes 33554448 | tf_op jit(solution)/shard_map/all_gather | solution.py:103
  777.8 17.2 %convolution_bitcast_fusion = f32[256,4096]{1,0:T(8,128)} fusion(bf16[4096,4096]{0,1:T(8,128)(2,1)} %all-gather.7.cloned.1.call-done, bf16[1,256,4096]{2,1,0:T(8,128)(2,1)S(1)} %copy-done), kind=kOutput, calls=%fused_computation.4 | convolution fusion | flops 8589934592 | bytes 39845888 | tf_op jit(solution)/shard_map/td,cd->tc/dot_general | solution.py:107
  795.0 6.7 fusion.29
  806.1 41.7 %copy.62 = bf16[32,8,128,256]{3,1,2,0:T(8,128)(2,1)S(1)} copy(bf16[32,8,128,256]{3,2,1,0:T(8,128)(2,1)S(1)} %bitcast.104) | data formatting | bytes 33554432
  847.8 6.5 slice.54
  854.3 56.7 %reshape.85 = bf16[256,128,255,1]{2,1,0,3:T(8,128)(2,1)} reshape(bf16[256,32640]{1,0:T(8,128)(2,1)} %slice.54) | data formatting | bytes 33423360 | tf_op jit(solution)/shard_map/reshape | solution.py:48
  911.1 56.7 %reshape.76 = bf16[256,128,255]{2,1,0:T(8,128)(2,1)} reshape(bf16[256,32640]{1,0:T(8,128)(2,1)} %slice.54) | data formatting | bytes 33423360 | tf_op jit(solution)/shard_map/reshape | solution.py:48
  967.8 2.3 fusion.39
  970.1 2.3 copy.59
  972.5 2.8 concatenate.56.clone
  975.3 12.2 convolution_bitcast_fusion.1
  987.5 3.5 slice.57
  991.0 3.0 copy.52
  995.3 2.4 convolution_convert_fusion
  999.4 18.3 %fusion.43 = f32[256,4096]{1,0:T(8,128)} fusion(bf16[256,4096]{1,0:T(8,128)(2,1)} %copy-done.6, bf16[4096,4096]{0,1:T(8,128)(2,1)} %all-gather.7.cloned.1.call-done), kind=kOutput, calls=%fused_computation.55 | convolution fusion | flops 8589934592 | bytes 39845888 | tf_op jit(solution)/shard_map/dot_general | solution.py:105
  1017.6 4.1 copy.46
  1021.7 4.0 concatenate.49
  1025.7 3.3 copy.48
  1030.7 4.2 copy.58
  1034.9 6.1 reshape.83
  1041.0 5.8 reduce_sum.9
  1046.9 9.9 fusion.24
  1056.8 2.2 copy.50
  1058.9 2.3 copy.72
  1061.2 6.0 copy.53
  1067.2 4.4 fusion.7
  1071.6 6.5 fusion.30
  1078.1 161.7 %all-reduce.8 = bf16[64,1024]{1,0:T(8,128)(2,1)} all-reduce(f32[64,1024]{1,0:T(8,128)} %reduce-scatter.5.cloned.1.call-done), channel_id=1, replica_groups=mesh['fsdp'=4,'ctx'=32] {'ctx'}, use_global_device_ids=true, to_apply=%region_2.3 | all-reduce | flops 65536 | bytes 393216 | tf_op jit(solution)/shard_map/psum | solution.py:144
  (64 shorter events, 16.2 us)
Async XLA Ops:
  7.2 254.0 %copy-start = (bf16[1,256,4096]{2,1,0:T(8,128)(2,1)S(1)}, bf16[1,256,4096]{2,1,0:T(8,128)(2,1)}, u32[]{:S(2)}) copy-start(bf16[1,256,4096]{2,1,0:T(8,128)(2,1)} %param.14) | copy-start | bytes 6291460
  7.2 26.8 %all-gather.5.cloned.1.call-start = ((), (), s32[]{:S(2)}) async-start(), calls=%async_computation.2 | async-start | bytes 1310720 | tf_op jit(solution)/shard_map/all_gather | solution.py:97
  10.6 767.2 %all-gather.7.cloned.1.call-start = ((), (), s32[]{:S(2)}) async-start(), calls=%async_computation.3 | async-start | bytes 34603008 | tf_op jit(solution)/shard_map/all_gather | solution.py:103
  34.0 1000.9 %all-gather.9.cloned.1.call-start = ((), (), s32[]{:S(2)}) async-start(), calls=%async_computation.5 | async-start | bytes 5242880 | tf_op jit(solution)/shard_map/all_gather | solution.py:141
  37.1 5.0 copy-start.3
  37.1 6.8 copy-start.12
  38.6 223.3 %collective-permute-start = (bf16[127,4096]{1,0:T(8,128)(2,1)}, bf16[127,4096]{1,0:T(8,128)(2,1)}, u32[]{:S(2)}, u32[]{:S(2)}) collective-permute-start(bf16[127,4096]{1,0:T(8,128)(2,1)} %slice.49), channel_id=1, source_target_pairs={{0,1},{1,2},{2,3},{3,4},{4,5},{5,6},{6,7},{7,8},{8,9},{9,10},{10,1... | collective-permute-start | bytes 3121160 | tf_op jit(solution)/shard_map/ppermute | solution.py:32
  150.4 7.3 copy-start.13
  150.4 19.3 %copy-start.15 = (bf16[128,64]{0,1:T(8,128)(2,1)S(1)}, bf16[128,64]{0,1:T(8,128)(2,1)}, u32[]{:S(2)}) copy-start(bf16[128,64]{0,1:T(8,128)(2,1)} %param.20) | copy-start | bytes 49156
  157.7 104.2 %copy-start.4 = (bf16[256,4096]{1,0:T(8,128)(2,1)S(1)}, bf16[256,4096]{1,0:T(8,128)(2,1)}, u32[]{:S(2)}) copy-start(bf16[256,4096]{1,0:T(8,128)(2,1)} %copy-done.3) | copy-start | bytes 6291460
  169.7 91.4 %copy-start.10 = (bf16[64,4096]{1,0:T(8,128)(2,1)}, bf16[64,4096]{1,0:T(8,128)(2,1)S(1)}, u32[]{:S(2)}) copy-start(bf16[64,4096]{1,0:T(8,128)(2,1)S(1)} %all_gather.21) | copy-start | bytes 1572868
  272.9 3.3 copy-start.7
  295.8 499.2 %copy-start.14 = (f32[4096]{0:T(1024)S(1)}, f32[4096]{0:T(1024)}, u32[]{:S(2)}) copy-start(f32[4096]{0:T(1024)} %param.19) | copy-start | bytes 49156
  777.8 17.2 %copy-start.5 = (bf16[256,4096]{1,0:T(8,128)(2,1)S(1)}, bf16[256,4096]{1,0:T(8,128)(2,1)}, u32[]{:S(2)}) copy-start(bf16[256,4096]{1,0:T(8,128)(2,1)} %copy-done.3) | copy-start | bytes 6291460
  777.8 17.2 %copy-start.9 = (f32[256,4096]{1,0:T(8,128)S(1)}, f32[256,4096]{1,0:T(8,128)}, u32[]{:S(2)}) copy-start(f32[256,4096]{1,0:T(8,128)} %copy.28) | copy-start | bytes 12582916
  801.7 1.3 copy-start.6
  804.6 273.6 %reduce-scatter.5.cloned.1.call-start = ((), (), s32[]{:S(2)}) async-start(), calls=%async_computation.6 | async-start | bytes 1310720 | tf_op jit(solution)/shard_map/reduce_scatter | solution.py:145
  911.1 56.7 %copy-start.16 = (pred[128]{0:T(512)(128)(4,1)S(1)}, pred[128]{0:T(512)(128)(4,1)}, u32[]{:S(2)}) copy-start(pred[128]{0:T(512)(128)(4,1)} %constant.31.clone.1) | copy-start | bytes 388
  994.0 77.7 %collective-permute-start.1 = (f32[127,4096]{1,0:T(8,128)}, f32[127,4096]{1,0:T(8,128)}, u32[]{:S(2)}, u32[]{:S(2)}) collective-permute-start(f32[127,4096]{1,0:T(8,128)} %copy.52), channel_id=1, source_target_pairs={{1,0},{2,1},{3,2},{4,3},{5,4},{6,5},{7,6},{8,7},{9,8},{10,9},{11,1... | collective-permute-start | bytes 6242312 | tf_op jit(solution)/shard_map/ppermute | solution.py:32
  999.1 240.7 %reduce-scatter.3.cloned.1.call-start = ((), (), s32[]{:S(2)}) async-start(), calls=%async_computation.4 | async-start | bytes 1081344 | tf_op jit(solution)/shard_map/reduce_scatter | solution.py:143
  1025.7 3.3 copy-start.1
  1061.2 6.0 copy-start.11
  1067.2 4.4 copy-start.2
  1067.2 4.4 copy-start.8
Sparse Core Ops, SparseCore 0:
  10.8 23.1 all-gather.4
  35.6 742.1 all-gather.6
  804.7 37.6 all-gather.8
  999.2 33.1 reduce-scatter.4
  1047.0 163.6 reduce-scatter.2
